TPU v7x, 32 devices: a whole 2x2x4 slice. The times are simulated.
32 devices in a mesh: dp: 8 (over z, y), ctx: 4 (over x, core).
Axes of the slice: x: 2, y: 2, z: 4, core: 2. Of those that a mesh axis runs over, the one named last changes fastest.
Arguments:
- projected: bfloat16 [8, 512, 3, 4096], P('dp', 'ctx'), may hold values from -6 to 6
- short_taps: float32 [3, 3, 4096], P(None, None, 'ctx'), may hold values from -3 to 3
- long_filter: bfloat16 [512, 4096], P('dp', 'ctx'), may hold values from -1.1 to 1.1
- skip_gain: float32 [4096], P('ctx'), may hold values from -4 to 4
Outputs:
- mixed: bfloat16 [8, 512, 4096], P('dp', 'ctx')
All inputs are finite; a program needn't handle non-finite values.
Results may differ from a plain program's by a relative error of at most 0.012.
Values may be sent and summed in bfloat16 or wider, within the bound.
A program may use at most 64 MiB of HBM per device.

v0:
```python
import math
import jax
import jax.numpy as jnp
import numpy as np
from jax import lax
from jax.sharding import PartitionSpec as P

RADIX = 64
HIGH = lax.Precision.HIGHEST


def causal_short(extended, taps, kernel_size):
    row_count = extended.shape[0] - (kernel_size - 1)
    widened = extended.astype(jnp.float32)
    summed = jnp.zeros((row_count,) + widened.shape[1:], jnp.float32)
    for tap_index in range(kernel_size):
        offset = kernel_size - 1 - tap_index
        summed = summed + taps[tap_index] * widened[offset : offset + row_count]
    return (summed[:, 0].astype(jnp.bfloat16), (summed[:, 1] * summed[:, 2]).astype(jnp.bfloat16))


def dft_tables(length, radix_size):
    outer_size = 2 * length // radix_size
    total_size = outer_size * radix_size
    outer_range = jnp.arange(outer_size, dtype=jnp.int32)
    inner_range = jnp.arange(radix_size, dtype=jnp.int32)
    angle_one = (
        2.0
        * math.pi
        / outer_size
        * (outer_range[:, None] * outer_range[None, :] % outer_size).astype(jnp.float32)
    )
    angle_twist = (
        2.0
        * math.pi
        / total_size
        * (outer_range[:, None] * inner_range[None, :] % total_size).astype(jnp.float32)
    )
    angle_two = (
        2.0
        * math.pi
        / radix_size
        * (inner_range[:, None] * inner_range[None, :] % radix_size).astype(jnp.float32)
    )
    twist_cos = jnp.cos(angle_twist)[:, :, None]
    twist_sin = jnp.sin(angle_twist)[:, :, None]
    return (
        jnp.cos(angle_one),
        jnp.sin(angle_one),
        twist_cos,
        twist_sin,
        jnp.cos(angle_two),
        jnp.sin(angle_two),
    )


def forward_dft(signal, tables, radix_size):
    cos_one, sin_one, twist_cos, twist_sin, cos_two, sin_two = tables
    outer_size = cos_one.shape[0]
    half_size = outer_size // 2
    block_width = signal.shape[1]
    shaped = signal.reshape(half_size, radix_size * block_width)
    first_re = jnp.dot(cos_one[:, :half_size], shaped, precision=HIGH).reshape(
        outer_size, radix_size, block_width
    )
    first_im = -jnp.dot(sin_one[:, :half_size], shaped, precision=HIGH).reshape(
        outer_size, radix_size, block_width
    )
    second_re = first_re * twist_cos + first_im * twist_sin
    second_im = first_im * twist_cos - first_re * twist_sin
    spec_re = jnp.einsum("amc,mb->abc", second_re, cos_two, precision=HIGH) + jnp.einsum(
        "amc,mb->abc", second_im, sin_two, precision=HIGH
    )
    spec_im = jnp.einsum("amc,mb->abc", second_im, cos_two, precision=HIGH) - jnp.einsum(
        "amc,mb->abc", second_re, sin_two, precision=HIGH
    )
    return (spec_re, spec_im)


def inverse_dft(spec_re, spec_im, tables, radix_size):
    cos_one, sin_one, twist_cos, twist_sin, cos_two, sin_two = tables
    outer_size = cos_one.shape[0]
    half_size = outer_size // 2
    block_width = spec_re.shape[2]
    back_re = jnp.einsum("abc,mb->amc", spec_re, cos_two, precision=HIGH) - jnp.einsum(
        "abc,mb->amc", spec_im, sin_two, precision=HIGH
    )
    back_im = jnp.einsum("abc,mb->amc", spec_re, sin_two, precision=HIGH) + jnp.einsum(
        "abc,mb->amc", spec_im, cos_two, precision=HIGH
    )
    turned_re = (back_re * twist_cos - back_im * twist_sin).reshape(
        outer_size, radix_size * block_width
    )
    turned_im = (back_re * twist_sin + back_im * twist_cos).reshape(
        outer_size, radix_size * block_width
    )
    result = jnp.dot(cos_one[:half_size], turned_re, precision=HIGH) - jnp.dot(
        sin_one[:half_size], turned_im, precision=HIGH
    )
    return result.reshape(half_size * radix_size, block_width) / (outer_size * radix_size)


def long_convolve_blocked(gated_slab, filter_slab):
    length, channels = gated_slab.shape
    block_width = min(128, channels)
    tables = dft_tables(length, RADIX)

    def one_block(block_index, output):
        offset = block_index * block_width
        signal = lax.dynamic_slice_in_dim(gated_slab, offset, block_width, 1).astype(jnp.float32)
        kernel_block = lax.dynamic_slice_in_dim(filter_slab, offset, block_width, 1).astype(
            jnp.float32
        )
        sig_re, sig_im = forward_dft(signal, tables, RADIX)
        ker_re, ker_im = forward_dft(kernel_block, tables, RADIX)
        prod_re = sig_re * ker_re - sig_im * ker_im
        prod_im = sig_re * ker_im + sig_im * ker_re
        result = inverse_dft(prod_re, prod_im, tables, RADIX)
        return lax.dynamic_update_slice_in_dim(output, result, offset, 1)

    return lax.fori_loop(
        0, channels // block_width, one_block, jnp.zeros((length, channels), jnp.float32)
    )


def long_convolve(gated_slab, filter_slab):
    length = gated_slab.shape[0]
    if length > 1024:
        return long_convolve_blocked(gated_slab, filter_slab)
    forward, backward = quarter_tables(length)
    sig = jnp.dot(forward, gated_slab, preferred_element_type=jnp.float32)
    ker = jnp.dot(forward, filter_slab, preferred_element_type=jnp.float32)
    sig_cos, sig_sin, ker_cos, ker_sin = (sig[:length], sig[length:], ker[:length], ker[length:])
    prod = jnp.concatenate(
        [sig_cos * ker_cos - sig_sin * ker_sin, sig_cos * ker_sin + sig_sin * ker_cos]
    ).astype(jnp.bfloat16)
    return jnp.dot(backward, prod, preferred_element_type=jnp.float32)


def quarter_tables(length):
    steps = (4 * np.arange(length)[:, None] + 1) * np.arange(length)[None, :] % (4 * length)
    angles = steps * (2.0 * math.pi / (4 * length))
    table = np.concatenate([np.cos(angles), np.sin(angles)])
    return (jnp.asarray(table, jnp.bfloat16), jnp.asarray(table.T / length, jnp.bfloat16))


def make_response(gated_slab, filter_slab, skip_gain):
    long_part = long_convolve(gated_slab, filter_slab)
    return (long_part + skip_gain * gated_slab.astype(jnp.float32)).astype(jnp.bfloat16)


def combine_rows(query_part, response_part):
    return (query_part.astype(jnp.float32) * response_part.astype(jnp.float32)).astype(jnp.bfloat16)


def on_device(projected, short_taps, long_filter, skip_gain):
    kernel_size = short_taps.shape[0]
    ctx_size = lax.axis_size("ctx")
    rows = projected[0]
    filter_slab = lax.all_gather(long_filter, "dp", axis=0, tiled=True)
    all_taps = lax.all_gather(short_taps, "ctx", axis=2, tiled=True)
    halo = lax.ppermute(
        rows[-(kernel_size - 1) :], "ctx", [(i, i + 1) for i in range(ctx_size - 1)]
    )
    queries, gated = causal_short(jnp.concatenate([halo, rows]), all_taps, kernel_size)
    gated_slab = lax.all_to_all(gated, "ctx", split_axis=1, concat_axis=0, tiled=True)
    response_slab = make_response(gated_slab, filter_slab, skip_gain)
    response = lax.all_to_all(response_slab, "ctx", split_axis=0, concat_axis=1, tiled=True)
    return combine_rows(queries, response)[None]


def solution(mesh):
    return jax.shard_map(
        on_device,
        mesh=mesh,
        in_specs=(P("dp", "ctx", None, None), P(None, None, "ctx"), P("dp", "ctx"), P("ctx")),
        out_specs=P("dp", "ctx", None),
        check_vma=False,
    )
```

profile of v0, /device:TPU:0, one launch (start us, length us, event | category | flops | bytes accessed | tf_op | source)
XLA Modules:
  0.0 98.3 jit_solution(9374394444664084530)
XLA Ops:
  6.5 0.0 all-gather.2.cloned.1.call-start
  6.5 1.0 slice_bitcast_fusion.3
  7.5 2.4 %collective-permute-start = (bf16[2,3,4096]{2,0,1:T(2,128)(2,1)S(1)}, bf16[2,3,4096]{2,0,1:T(2,128)(2,1)S(1)}, u32[]{:S(2)}, u32[]{:S(2)}) collective-permute-start(bf16[2,3,4096]{2,0,1:T(2,128)(2,1)S(1)} %slice_bitcast_fusion.3), channel_id=1, source_target_pairs={{0,1},{1,2},{2,3},{4,5},{5,6},{6,7},{8,9},{9,10},{10,11},{12,13},{... | collective-permute-start | bytes 147464 | tf_op jit(solution)/shard_map/ppermute | solution.py:162
  9.9 0.0 all-gather.2.cloned.1.call-update
  9.9 7.1 %all_gather.6 = f32[3,3,4096]{2,1,0:T(4,128)S(1)} all-gather(f32[3,3,1024]{2,1,0:T(4,128)} %param.7), channel_id=1, replica_groups=mesh['dp'=8,'ctx'=4] {'ctx'}, dimensions={2}, use_global_device_ids=true | all-gather | bytes 184320 | tf_op jit(solution)/shard_map/all_gather | solution.py:161
  17.1 3.5 %copy.19 = bf16[1,128,3,4096]{1,3,2,0:T(8,128)(2,1)S(1)} copy(bf16[1,128,3,4096]{3,1,2,0:T(8,128)(2,1)} %param.6) | data formatting | bytes 6291456 | tf_op args[0]
  20.6 0.0 collective-permute-done
  20.6 2.8 %copy.20 = bf16[2,3,4096]{0,2,1:T(8,128)(2,1)} copy(bf16[2,3,4096]{2,0,1:T(2,128)(2,1)S(1)} %collective-permute-done) | data formatting | bytes 98304 | tf_op jit(solution)/shard_map/ppermute | solution.py:162
  23.4 4.1 %maximum_convert_fusion = f32[130,3,4096]{0,2,1:T(8,128)S(1)} fusion(bf16[128,3,4096]{0,2,1:T(8,128)(2,1)S(1)} %bitcast.36, bf16[2,3,4096]{0,2,1:T(8,128)(2,1)} %copy.20), kind=kLoop, calls=%fused_computation.5 | loop fusion | flops 6389760 | bytes 9584640 | tf_op jit(solution)/shard_map/convert_element_type | solution.py:14
  27.5 9.4 %fusion = f32[128,3,4096]{0,2,1:T(8,128)S(1)} fusion(f32[130,3,4096]{0,2,1:T(8,128)S(1)} %maximum_convert_fusion, f32[3,4096]{1,0:T(4,128)S(1)} %get-tuple-element.6, f32[3,4096]{1,0:T(4,128)S(1)} %get-tuple-element.7, f32[3,4096]{1,0:T(4,128)S(1)} %get-tuple-element.5), kind=kLoop, calls=%fused_computation.1 | loop fusion | flops 7864320 | bytes 25313280 | tf_op jit(solution)/shard_map/add | solution.py:18
  36.9 0.0 copy-start
  36.9 2.7 %copy-done = f32[128,3,4096]{0,2,1:T(8,128)} copy-done((f32[128,3,4096]{0,2,1:T(8,128)}, f32[128,3,4096]{0,2,1:T(8,128)S(1)}, u32[]{:S(2)}) %copy-start) | copy-done | bytes 6291480
  39.5 0.2 fusion.2
  39.7 0.5 copy.21
  40.3 16.9 %all_to_all.29 = bf16[128,4,1024]{2,0,1:T(8,128)(2,1)S(1)} all-to-all(bf16[128,4,1024]{2,0,1:T(8,128)(2,1)S(1)} %copy.21), channel_id=1, replica_groups=mesh['dp'=8,'ctx'=4] {'ctx'}, dimensions={1} | all-to-all | bytes 2097152 | tf_op jit(solution)/shard_map/all_to_all | solution.py:166
  57.2 0.8 copy.22
  58.0 0.3 reshape.46
  58.3 4.5 %fusion.8 = f32[1024,1024]{1,0:T(8,128)} fusion(bf16[1024,512]{1,0:T(8,128)(2,1)} %constant.9, bf16[512,1024]{1,0:T(8,128)(2,1)S(1)} %reshape.46), kind=kOutput, calls=%fused_computation.23 | convolution fusion | flops 1073741824 | bytes 6291456 | tf_op jit(solution)/shard_map/dot_general | solution.py:131
  62.8 0.0 copy-start.3
  62.8 0.0 all-gather.2.cloned.1.call-done
  62.8 2.9 %fusion.9 = f32[1024,1024]{1,0:T(8,128)S(1)} fusion(bf16[1024,512]{1,0:T(8,128)(2,1)} %constant.4.clone, bf16[512,1024]{1,0:T(8,128)(2,1)} %all-gather.2.cloned.1.call-done), kind=kOutput, calls=%fused_computation.24 | convolution fusion | flops 1073741824 | bytes 6291456 | tf_op jit(solution)/shard_map/dot_general | solution.py:132
  65.7 0.0 copy-done.3
  65.7 0.0 copy-done.1
  65.8 0.8 fusion.6
  66.6 0.2 copy-done.2
  66.8 0.0 copy-done.4
  66.8 0.9 fusion.4
  67.7 16.9 %all_to_all.30 = bf16[4,128,1024]{2,1,0:T(8,128)(2,1)S(1)} all-to-all(bf16[4,128,1024]{2,1,0:T(8,128)(2,1)S(1)} %bitcast.38), channel_id=1, replica_groups=mesh['dp'=8,'ctx'=4] {'ctx'}, dimensions={0} | all-to-all | bytes 2097152 | tf_op jit(solution)/shard_map/all_to_all | solution.py:168
  84.6 1.6 %convert_bitcast_fusion = f32[128,4,1024]{2,0,1:T(8,128)} fusion(bf16[4,128,1024]{2,1,0:T(8,128)(2,1)S(1)} %all_to_all.30), kind=kLoop, calls=%fused_computation.14 | loop fusion | flops 524288 | bytes 3145728 | tf_op jit(solution)/shard_map/convert_element_type | solution.py:153
  86.1 1.9 %copy.23 = f32[128,4,1024]{0,2,1:T(8,128)S(1)} copy(f32[128,4,1024]{2,0,1:T(8,128)} %convert_bitcast_fusion) | data formatting | bytes 4194304 | tf_op jit(solution)/shard_map/convert_element_type | solution.py:153
  88.1 2.0 %fusion.5 = bf16[1,128,4096]{1,2,0:T(8,128)(2,1)S(1)} fusion(f32[128,4,1024]{0,2,1:T(8,128)S(1)} %copy.23, f32[128,3,4096]{0,2,1:T(8,128)} %copy-done), kind=kLoop, calls=%fused_computation.13 | loop fusion | flops 1572864 | bytes 4194304 | tf_op jit(solution)/shard_map/convert_element_type | solution.py:153
  90.1 1.3 %copy.24 = bf16[1,128,4096]{2,1,0:T(8,128)(2,1)} copy(bf16[1,128,4096]{1,2,0:T(8,128)(2,1)S(1)} %fusion.5) | data formatting | bytes 2097152 | tf_op jit(solution)/shard_map/convert_element_type | solution.py:153
  (4 shorter events, 0.0 us)
Async XLA Ops:
  6.5 56.2 %all-gather.2.cloned.1.call-start = ((), (), s32[]{:S(2)}) async-start(), calls=%async_computation.2 | async-start | bytes 1179648 | tf_op jit(solution)/shard_map/all_gather | solution.py:160
  7.5 13.0 %collective-permute-start = (bf16[2,3,4096]{2,0,1:T(2,128)(2,1)S(1)}, bf16[2,3,4096]{2,0,1:T(2,128)(2,1)S(1)}, u32[]{:S(2)}, u32[]{:S(2)}) collective-permute-start(bf16[2,3,4096]{2,0,1:T(2,128)(2,1)S(1)} %slice_bitcast_fusion.3), channel_id=1, source_target_pairs={{0,1},{1,2},{2,3},{4,5},{5,6},{6,7},{8,9},{9,10},{10,11},{12,13},{... | collective-permute-start | bytes 147464 | tf_op jit(solution)/shard_map/ppermute | solution.py:162
  36.9 2.7 %copy-start = (f32[128,3,4096]{0,2,1:T(8,128)}, f32[128,3,4096]{0,2,1:T(8,128)S(1)}, u32[]{:S(2)}) copy-start(f32[128,3,4096]{0,2,1:T(8,128)S(1)} %fusion) | copy-start | bytes 18874372
  62.8 3.0 %copy-start.3 = (bf16[512,512]{1,0:T(8,128)(2,1)S(1)}, bf16[512,512]{1,0:T(8,128)(2,1)}, u32[]{:S(2)}) copy-start(bf16[512,512]{1,0:T(8,128)(2,1)} %constant.10) | copy-start | bytes 1572868
  62.8 3.0 %copy-start.1 = (f32[1024,1024]{1,0:T(8,128)S(1)}, f32[1024,1024]{1,0:T(8,128)}, u32[]{:S(2)}) copy-start(f32[1024,1024]{1,0:T(8,128)} %fusion.8) | copy-start | bytes 12582916
  65.8 1.0 %copy-start.2 = (bf16[512,512]{1,0:T(8,128)(2,1)S(1)}, bf16[512,512]{1,0:T(8,128)(2,1)}, u32[]{:S(2)}) copy-start(bf16[512,512]{1,0:T(8,128)(2,1)} %constant.11) | copy-start | bytes 1572868
  65.8 1.0 %copy-start.4 = (f32[1024]{0:T(1024)S(1)}, f32[1024]{0:T(1024)}, u32[]{:S(2)}) copy-start(f32[1024]{0:T(1024)} %param.9) | copy-start | bytes 12292
Sparse Core Ops, SparseCore 0:
  10.0 42.7 all-gather.1
where the time goes:
time: 98.7 us; the launch traced here: 98.3 us
  blocking collectives  40.9 us (41%)
  other arithmetic  17.3 us (18%)
  local copies, waits for them, and re-layouts  15.1 us (15%)
  between operations  13.5 us (14%)
  matrix products  9.08 us (9%)
  starting transfers between devices  2.36 us (2%)
    all_to_all x1, blocking collectives, on_device(): lax.all_to_all(gated, 'ctx', split_axis=1, concat_axis=0, tiled=True)  16.9 us
    all_to_all x1, blocking collectives, on_device(): lax.all_to_all(response_slab, 'ctx', split_axis=0, concat_axis=1, tiled=T...  16.9 us
    add x1, other arithmetic, causal_short(): summed = summed + taps[tap_index] * widened[offset:offset + row_count]  9.39 us
    all_gather x1, blocking collectives, on_device(): all_taps = lax.all_gather(short_taps, 'ctx', axis=2, tiled=True)  7.11 us
    unnamed x11, local copies, waits for them, and re-layouts  6.44 us
    dot_general x1, matrix products, long_convolve(): sig = jnp.dot(forward, gated_slab, preferred_element_type=jnp.float32)  4.5 us
    convert_element_type x1, other arithmetic, causal_short(): widened = extended.astype(jnp.float32)  4.08 us
    dot_general x1, matrix products, long_convolve(): ker = jnp.dot(forward, filter_slab, preferred_element_type=jnp.float32)  2.94 us
  transfers between devices with their start and end apart: 2, of which 0 were waited for; matrix products, arithmetic and copies ran while one was open for 27% of the time, Pallas kernels for 0%

commit v1 on v0

--- a/solution.py
+++ b/solution.py
@@ -158,7 +158,12 @@
     ctx_size = lax.axis_size("ctx")
     rows = projected[0]
     filter_slab = lax.all_gather(long_filter, "dp", axis=0, tiled=True)
-    all_taps = lax.all_gather(short_taps, "ctx", axis=2, tiled=True)
+    ring = [short_taps]
+    for hop in range(3):
+        ring.append(lax.ppermute(ring[-1], "ctx", [(dev, (dev + 1) % 4) for dev in range(4)]))
+    all_taps = jnp.roll(
+        jnp.concatenate(ring[::-1], axis=2), (lax.axis_index("ctx") + 1) * ring[0].shape[2], axis=2
+    )
     halo = lax.ppermute(
         rows[-(kernel_size - 1) :], "ctx", [(i, i + 1) for i in range(ctx_size - 1)]
     )

time: 98.7 us -> 95.2 us (0.965)
  blocking collectives: 40.9 us -> 33.8 us
  starting transfers between devices: 2.36 us -> 5.78 us
    all_gather x1 -> x0, blocking collectives: 7.11 us -> none  [on_device(): all_taps = lax.all_gather(short_taps, 'ctx', axis=2, tiled=True)]
    ppermute x1, starting transfers between devices: 2.36 us -> 4.51 us  [on_device(): lax.ppermute(rows[-(kernel_size - 1):], 'ctx', [(i, i + 1) for i in range...]
    ppermute x0 -> x3, starting transfers between devices: none -> 1.27 us  [on_device(): lax.ppermute(ring[-1], 'ctx', [(dev, (dev + 1) % 4) for dev in range(4)])]
    unnamed x11 -> x20, local copies, waits for them, and re-layouts: 6.44 us -> 6.52 us
  transfers between devices with their start and end apart: 2 -> 5, of which waited for: 0 -> 0; matrix products, arithmetic and copies ran while one was open for 27% -> 29% of each run, Pallas kernels for 0% -> 0%
where the time goes in v1:
time: 95.2 us; the launch traced here: 94.8 us
  blocking collectives  33.8 us (36%)
  other arithmetic  17.3 us (18%)
  local copies, waits for them, and re-layouts  15.2 us (16%)
  between operations  13.6 us (14%)
  matrix products  9.08 us (10%)
  starting transfers between devices  5.78 us (6%)
    all_to_all x1, blocking collectives, on_device(): lax.all_to_all(gated, 'ctx', split_axis=1, concat_axis=0, tiled=True)  16.9 us
    all_to_all x1, blocking collectives, on_device(): lax.all_to_all(response_slab, 'ctx', split_axis=0, concat_axis=1, tiled=T...  16.9 us
    add x1, other arithmetic, causal_short(): summed = summed + taps[tap_index] * widened[offset:offset + row_count]  9.39 us
    unnamed x20, local copies, waits for them, and re-layouts  6.52 us
    ppermute x1, starting transfers between devices, on_device(): lax.ppermute(rows[-(kernel_size - 1):], 'ctx', [(i, i + 1) for i in range...  4.51 us
    dot_general x1, matrix products, long_convolve(): sig = jnp.dot(forward, gated_slab, preferred_element_type=jnp.float32)  4.5 us
    convert_element_type x1, other arithmetic, causal_short(): widened = extended.astype(jnp.float32)  4.11 us
    dot_general x1, matrix products, long_convolve(): ker = jnp.dot(forward, filter_slab, preferred_element_type=jnp.float32)  2.94 us
  transfers between devices with their start and end apart: 5, of which 0 were waited for; matrix products, arithmetic and copies ran while one was open for 29% of the time, Pallas kernels for 0%

profile of v1, /device:TPU:0, one launch (start us, length us, event | category | flops | bytes accessed | tf_op | source)
XLA Modules:
  0.0 94.8 jit_solution(11134149246168826643)
XLA Ops:
  6.5 0.5 collective-permute-start
  7.0 1.0 %slice_bitcast_fusion = bf16[2,3,4096]{2,0,1:T(2,128)(2,1)S(1)} fusion(bf16[1,128,3,4096]{3,1,2,0:T(8,128)(2,1)} %param.6), kind=kLoop, calls=%fused_computation.22 | loop fusion | bytes 98304 | tf_op jit(solution)/shard_map/slice | solution.py:168
  8.0 4.5 %collective-permute-start.3 = (bf16[2,3,4096]{2,0,1:T(2,128)(2,1)S(1)}, bf16[2,3,4096]{2,0,1:T(2,128)(2,1)S(1)}, u32[]{:S(2)}, u32[]{:S(2)}) collective-permute-start(bf16[2,3,4096]{2,0,1:T(2,128)(2,1)S(1)} %slice_bitcast_fusion), channel_id=1, source_target_pairs={{0,1},{1,2},{2,3},{4,5},{5,6},{6,7},{8,9},{9,10},{10,11},{12,13},{... | collective-permute-start | bytes 147464 | tf_op jit(solution)/shard_map/ppermute | solution.py:167
  12.5 0.0 collective-permute-done
  12.5 0.1 collective-permute-start.1
  12.6 0.0 all-gather.2.cloned.1.call-update
  12.6 3.5 %copy.19 = bf16[1,128,3,4096]{1,3,2,0:T(8,128)(2,1)S(1)} copy(bf16[1,128,3,4096]{3,1,2,0:T(8,128)(2,1)} %param.6) | data formatting | bytes 6291456 | tf_op args[0]
  16.1 0.0 collective-permute-done.3
  16.1 2.8 %copy.20 = bf16[2,3,4096]{0,2,1:T(8,128)(2,1)} copy(bf16[2,3,4096]{2,0,1:T(2,128)(2,1)S(1)} %collective-permute-done.3) | data formatting | bytes 98304 | tf_op jit(solution)/shard_map/ppermute | solution.py:167
  18.9 0.0 collective-permute-done.1
  18.9 0.8 collective-permute-start.2
  19.7 4.1 %maximum_convert_fusion = f32[130,3,4096]{0,2,1:T(8,128)S(1)} fusion(bf16[128,3,4096]{0,2,1:T(8,128)(2,1)S(1)} %bitcast.36, bf16[2,3,4096]{0,2,1:T(8,128)(2,1)} %copy.20), kind=kLoop, calls=%fused_computation.5 | loop fusion | flops 6389760 | bytes 9584640 | tf_op jit(solution)/shard_map/convert_element_type | solution.py:14
  23.8 0.0 collective-permute-done.2
  24.0 9.4 %fusion = f32[128,3,4096]{0,2,1:T(8,128)S(1)} fusion(f32[130,3,4096]{0,2,1:T(8,128)S(1)} %maximum_convert_fusion, f32[3,4096]{1,0:T(4,128)S(1)} %get-tuple-element.7, f32[3,4096]{1,0:T(4,128)S(1)} %get-tuple-element.6, f32[3,4096]{1,0:T(4,128)S(1)} %get-tuple-element.5), kind=kLoop, calls=%fused_computation.1 | loop fusion | flops 7864320 | bytes 25313280 | tf_op jit(solution)/shard_map/add | solution.py:18
  33.5 2.6 %copy-done = f32[128,3,4096]{0,2,1:T(8,128)} copy-done((f32[128,3,4096]{0,2,1:T(8,128)}, f32[128,3,4096]{0,2,1:T(8,128)S(1)}, u32[]{:S(2)}) %copy-start) | copy-done | bytes 6291480
  36.1 0.2 fusion.2
  36.3 0.5 copy.21
  36.8 16.9 %all_to_all.29 = bf16[128,4,1024]{2,0,1:T(8,128)(2,1)S(1)} all-to-all(bf16[128,4,1024]{2,0,1:T(8,128)(2,1)S(1)} %copy.21), channel_id=1, replica_groups=mesh['dp'=8,'ctx'=4] {'ctx'}, dimensions={1} | all-to-all | bytes 2097152 | tf_op jit(solution)/shard_map/all_to_all | solution.py:171
  53.7 0.8 copy.22
  54.5 0.3 reshape.46
  54.8 4.5 %fusion.8 = f32[1024,1024]{1,0:T(8,128)} fusion(bf16[1024,512]{1,0:T(8,128)(2,1)} %constant.39, bf16[512,1024]{1,0:T(8,128)(2,1)S(1)} %reshape.46), kind=kOutput, calls=%fused_computation.31 | convolution fusion | flops 1073741824 | bytes 6291456 | tf_op jit(solution)/shard_map/dot_general | solution.py:131
  59.3 2.9 %fusion.9 = f32[1024,1024]{1,0:T(8,128)S(1)} fusion(bf16[1024,512]{1,0:T(8,128)(2,1)} %constant.34.clone, bf16[512,1024]{1,0:T(8,128)(2,1)} %all-gather.2.cloned.1.call-done), kind=kOutput, calls=%fused_computation.32 | convolution fusion | flops 1073741824 | bytes 6291456 | tf_op jit(solution)/shard_map/dot_general | solution.py:132
  62.3 0.0 copy-done.1
  62.3 0.8 fusion.6
  63.1 0.2 copy-done.2
  63.4 0.0 copy-done.5
  63.4 0.9 fusion.4
  64.2 16.9 %all_to_all.30 = bf16[4,128,1024]{2,1,0:T(8,128)(2,1)S(1)} all-to-all(bf16[4,128,1024]{2,1,0:T(8,128)(2,1)S(1)} %bitcast.38), channel_id=1, replica_groups=mesh['dp'=8,'ctx'=4] {'ctx'}, dimensions={0} | all-to-all | bytes 2097152 | tf_op jit(solution)/shard_map/all_to_all | solution.py:173
  81.1 1.6 %convert_bitcast_fusion = f32[128,4,1024]{2,0,1:T(8,128)} fusion(bf16[4,128,1024]{2,1,0:T(8,128)(2,1)S(1)} %all_to_all.30), kind=kLoop, calls=%fused_computation.14 | loop fusion | flops 524288 | bytes 3145728 | tf_op jit(solution)/shard_map/convert_element_type | solution.py:153
  82.7 1.9 %copy.23 = f32[128,4,1024]{0,2,1:T(8,128)S(1)} copy(f32[128,4,1024]{2,0,1:T(8,128)} %convert_bitcast_fusion) | data formatting | bytes 4194304 | tf_op jit(solution)/shard_map/convert_element_type | solution.py:153
  84.6 2.0 %fusion.5 = bf16[1,128,4096]{1,2,0:T(8,128)(2,1)S(1)} fusion(f32[128,4,1024]{0,2,1:T(8,128)S(1)} %copy.23, f32[128,3,4096]{0,2,1:T(8,128)} %copy-done), kind=kLoop, calls=%fused_computation.13 | loop fusion | flops 1572864 | bytes 4194304 | tf_op jit(solution)/shard_map/convert_element_type | solution.py:153
  86.7 1.3 %copy.24 = bf16[1,128,4096]{2,1,0:T(8,128)(2,1)} copy(bf16[1,128,4096]{1,2,0:T(8,128)(2,1)S(1)} %fusion.5) | data formatting | bytes 2097152 | tf_op jit(solution)/shard_map/convert_element_type | solution.py:153
  (19 shorter events, 0.2 us)
Async XLA Ops:
  6.5 52.8 %all-gather.2.cloned.1.call-start = ((), (), s32[]{:S(2)}) async-start(), calls=%async_computation.2 | async-start | bytes 1179648 | tf_op jit(solution)/shard_map/all_gather | solution.py:160
  6.5 6.0 %collective-permute-start = (f32[3,3,1024]{2,1,0:T(4,128)}, f32[3,3,1024]{2,1,0:T(4,128)S(1)}, u32[]{:S(2)}, u32[]{:S(2)}) collective-permute-start(f32[3,3,1024]{2,1,0:T(4,128)} %param.7), channel_id=1, source_target_pairs={{0,1},{1,2},{2,3},{3,0},{4,5},{5,6},{6,7},{7,4},{8,9},{9,10},{10,1... | collective-permute-start | bytes 110600 | tf_op jit(solution)/shard_map/ppermute | solution.py:163
  8.0 8.1 %collective-permute-start.3 = (bf16[2,3,4096]{2,0,1:T(2,128)(2,1)S(1)}, bf16[2,3,4096]{2,0,1:T(2,128)(2,1)S(1)}, u32[]{:S(2)}, u32[]{:S(2)}) collective-permute-start(bf16[2,3,4096]{2,0,1:T(2,128)(2,1)S(1)} %slice_bitcast_fusion), channel_id=1, source_target_pairs={{0,1},{1,2},{2,3},{4,5},{5,6},{6,7},{8,9},{9,10},{10,11},{12,13},{... | collective-permute-start | bytes 147464 | tf_op jit(solution)/shard_map/ppermute | solution.py:167
  12.5 6.4 %collective-permute-start.1 = (f32[3,3,1024]{2,1,0:T(4,128)S(1)}, f32[3,3,1024]{2,1,0:T(4,128)S(1)}, u32[]{:S(2)}, u32[]{:S(2)}) collective-permute-start(f32[3,3,1024]{2,1,0:T(4,128)S(1)} %collective-permute-done), channel_id=1, source_target_pairs={{0,1},{1,2},{2,3},{3,0},{4,5},{5,6},{6,7},{7,4},{8,9},{9,10},{10,1... | collective-permute-start | bytes 110600 | tf_op jit(solution)/shard_map/ppermute | solution.py:163
  18.9 4.9 %collective-permute-start.2 = (f32[3,3,1024]{2,1,0:T(4,128)S(1)}, f32[3,3,1024]{2,1,0:T(4,128)S(1)}, u32[]{:S(2)}, u32[]{:S(2)}) collective-permute-start(f32[3,3,1024]{2,1,0:T(4,128)S(1)} %collective-permute-done.1), channel_id=1, source_target_pairs={{0,1},{1,2},{2,3},{3,0},{4,5},{5,6},{6,7},{7,4},{8,9},{9,10},{10,1... | collective-permute-start | bytes 110600 | tf_op jit(solution)/shard_map/ppermute | solution.py:163
  19.7 4.2 %copy-start.4 = (f32[3,3,1024]{2,1,0:T(4,128)S(1)}, f32[3,3,1024]{2,1,0:T(4,128)}, u32[]{:S(2)}) copy-start(f32[3,3,1024]{2,1,0:T(4,128)} %param.7) | copy-start | bytes 110596
  33.4 2.6 %copy-start = (f32[128,3,4096]{0,2,1:T(8,128)}, f32[128,3,4096]{0,2,1:T(8,128)S(1)}, u32[]{:S(2)}) copy-start(f32[128,3,4096]{0,2,1:T(8,128)S(1)} %fusion) | copy-start | bytes 18874372
  59.3 3.0 %copy-start.3 = (bf16[512,512]{1,0:T(8,128)(2,1)S(1)}, bf16[512,512]{1,0:T(8,128)(2,1)}, u32[]{:S(2)}) copy-start(bf16[512,512]{1,0:T(8,128)(2,1)} %constant.40) | copy-start | bytes 1572868
  59.3 3.0 %copy-start.1 = (f32[1024,1024]{1,0:T(8,128)S(1)}, f32[1024,1024]{1,0:T(8,128)}, u32[]{:S(2)}) copy-start(f32[1024,1024]{1,0:T(8,128)} %fusion.8) | copy-start | bytes 12582916
  62.3 1.0 %copy-start.2 = (bf16[512,512]{1,0:T(8,128)(2,1)S(1)}, bf16[512,512]{1,0:T(8,128)(2,1)}, u32[]{:S(2)}) copy-start(bf16[512,512]{1,0:T(8,128)(2,1)} %constant.41) | copy-start | bytes 1572868
  62.3 1.0 %copy-start.5 = (f32[1024]{0:T(1024)S(1)}, f32[1024]{0:T(1024)}, u32[]{:S(2)}) copy-start(f32[1024]{0:T(1024)} %param.9) | copy-start | bytes 12292
Sparse Core Ops, SparseCore 0:
  12.7 41.7 all-gather.1
